TPU v7x, 32 devices: a whole 2x2x4 slice. The times are simulated.
32 devices in a mesh: tile: 8 (over z, y), clip: 4 (over x, core).
Axes of the slice: x: 2, y: 2, z: 4, core: 2. Of those that a mesh axis runs over, the one named last changes fastest.
Arguments:
- seq_rows: bfloat16 [32768, 512], P(('tile', 'clip'))
- plan_owner: int32 [32768], P(('tile', 'clip')), may hold values from 0 to 31, as said below
- plan_slot: int32 [32768], P(('tile', 'clip')), may hold values from 0 to 1023, as said below
- live_frames: int32 [4], replicated, may hold values from 1 to 4, as said below
- norm_gain: float32 [512], replicated, may hold values from 0.1 to 1.9
- norm_bias: float32 [512], replicated, may hold values from -3 to 3
- conv_weight: bfloat16 [3, 3, 512, 3, 256], replicated, may hold values from -0.0546875 to 0.0546875
- conv_bias: float32 [256], replicated, may hold values from -3 to 3
Outputs:
- decoded: bfloat16 [4, 8, 4, 8, 32, 256], P('clip', 'tile')
Inputs may be any that keep to these rules, and one draw needn't show every extreme that they name: `plan_owner`: owner o is tile o % 8 of clip o // 8. The 1024 rows of each device send 32 // 2 or 48 rows to each owner, so at most 48, which is reached. The pairs of plan_owner and plan_slot are all distinct: every slot of every owner receives exactly one row. `live_frames`: some clip has all 4 frames live.
All inputs are finite; a program needn't handle non-finite values.
Results may differ from a plain program's by a relative error of at most 0.004.
Values may be sent and summed in bfloat16 or wider, within the bound.
A program may use at most 128 MiB of HBM per device.

v0:
```python
import jax
import jax.numpy as jnp
from jax import lax
from jax.sharding import PartitionSpec as P

GROUPS = 32
LT = 4
TH = 8
TW = 32
GW = 4
EPSILON = 1e-06
HIGHEST = lax.Precision.HIGHEST


def shifted(block, axis, distance):
    devices = range(lax.axis_size(axis))
    route = [(i - distance, i) for i in devices if i - distance in devices]
    return lax.ppermute(block, axis, route)


def neighbour(values, offset):
    return shifted(values, "tile", offset)


def extend(tile_grid, column_tile, grid_cols):
    left_face = neighbour(tile_grid[:, :, -1:], 1)
    right_face = neighbour(tile_grid[:, :, :1], -1)
    left_face = jnp.where(column_tile > 0, left_face, jnp.zeros_like(left_face))
    right_face = jnp.where(column_tile < grid_cols - 1, right_face, jnp.zeros_like(right_face))
    widened = jnp.concatenate([left_face, tile_grid, right_face], axis=2)
    upper_face = neighbour(widened[:, -1:], grid_cols)
    lower_face = neighbour(widened[:, :1], -grid_cols)
    return jnp.concatenate([upper_face, widened, lower_face], axis=1)


def normalize(values, mean_channel, scale_channel, norm_gain, norm_bias):
    normed = (values.astype(jnp.float32) - mean_channel) * scale_channel * norm_gain + norm_bias
    return jax.nn.silu(normed)


def on_device(
    seq_rows, plan_owner, plan_slot, live_frames, norm_gain, norm_bias, conv_weight, conv_bias
):
    row_count, channels = seq_rows.shape
    out_width = conv_bias.shape[0]
    tile_count = lax.axis_size("tile")
    clip_count = lax.axis_size("clip")
    owner_count = tile_count * clip_count
    capacity = 3 * (row_count // owner_count) // 2
    per_group = channels // GROUPS
    plane_size = TH * TW
    voxel_total = float(plane_size * tile_count)
    row_index = jnp.arange(row_count, dtype=jnp.int32)
    owner_table = (plan_owner[:, None] == jnp.arange(owner_count, dtype=jnp.int32)[None, :]).astype(
        jnp.int32
    )
    ranking = jnp.sum((jnp.cumsum(owner_table, axis=0) - 1) * owner_table, axis=1)
    position = plan_owner * capacity + ranking
    my_clip = lax.axis_index("clip")
    my_tile = lax.axis_index("tile")
    frames_live = live_frames[my_clip]
    outgoing = (
        jnp.zeros((owner_count * capacity, channels), jnp.bfloat16).at[position].set(seq_rows)
    )
    slot_list = (
        jnp.full((owner_count * capacity,), row_count, jnp.int32).at[position].set(plan_slot)
    )
    outgoing = outgoing.reshape(clip_count, tile_count, capacity, channels)
    slot_list = slot_list.reshape(clip_count, tile_count, capacity)
    arrived, arrived_slots = (
        lax.all_to_all(
            lax.all_to_all(outgoing, "tile", split_axis=1, concat_axis=1, tiled=True),
            "clip",
            split_axis=0,
            concat_axis=0,
            tiled=True,
        ),
        lax.all_to_all(
            lax.all_to_all(slot_list, "tile", split_axis=1, concat_axis=1, tiled=True),
            "clip",
            split_axis=0,
            concat_axis=0,
            tiled=True,
        ),
    )
    tile_rows = (
        jnp.zeros((row_count, channels), jnp.bfloat16)
        .at[arrived_slots.reshape(-1)]
        .set(arrived.reshape(-1, channels), mode="drop")
    )
    grid_cols = GW
    grid_rows = tile_count // grid_cols
    column_tile = my_tile % grid_cols
    row_tile = my_tile // grid_cols
    live_frame = jnp.arange(LT) < frames_live
    values = tile_rows.astype(jnp.float32)
    live_row = (row_index // plane_size < frames_live).astype(jnp.float32)
    first_sum = jnp.dot(live_row, values, precision=HIGHEST).reshape(GROUPS, per_group).sum(axis=1)
    second_sum = (
        jnp.dot(live_row, values * values, precision=HIGHEST).reshape(GROUPS, per_group).sum(axis=1)
    )
    raw_padded = extend(tile_rows.reshape(LT, TH, TW, channels), column_tile, grid_cols)
    first_sum, second_sum = lax.psum((first_sum, second_sum), "tile")
    count_clip = per_group * frames_live.astype(jnp.float32) * voxel_total
    mean_group = first_sum / count_clip
    scale_group = lax.rsqrt(second_sum / count_clip - mean_group * mean_group + EPSILON)
    mean_channel = jnp.repeat(mean_group, per_group)
    scale_channel = jnp.repeat(scale_group, per_group)
    inside_rows = jnp.arange(TH + 2)
    inside_cols = jnp.arange(TW + 2)
    rows_inside = ((inside_rows > 0) | (row_tile > 0)) & (
        (inside_rows < TH + 1) | (row_tile < grid_rows - 1)
    )
    cols_inside = ((inside_cols > 0) | (column_tile > 0)) & (
        (inside_cols < TW + 1) | (column_tile < grid_cols - 1)
    )
    valid_mask = rows_inside[:, None] & cols_inside[None, :]
    activated = normalize(raw_padded, mean_channel, scale_channel, norm_gain, norm_bias)
    padded = jnp.where(valid_mask[None, :, :, None], activated, 0.0).astype(jnp.bfloat16)
    padded = jnp.concatenate(
        [jnp.zeros((2, TH + 2, TW + 2, channels), jnp.bfloat16), padded], axis=0
    )
    accumulated = jnp.zeros((LT, TH, TW, out_width), jnp.float32)
    for tap_t in range(3):
        for tap_h in range(3):
            slab_rows = padded[tap_t : tap_t + LT, tap_h : tap_h + TH].reshape(-1, channels)
            kernel = conv_weight[tap_t, tap_h].reshape(channels, 3 * out_width)
            product = jnp.dot(slab_rows, kernel, preferred_element_type=jnp.float32)
            product = product.reshape(LT, TH, TW + 2, 3, out_width)
            for tap_w in range(3):
                accumulated = accumulated + product[:, :, tap_w : tap_w + TW, tap_w]
    decoded = jnp.where(live_frame[:, None, None, None], accumulated + conv_bias, 0.0)
    return decoded.astype(jnp.bfloat16)[None, None]


def solution(mesh):
    return jax.shard_map(
        on_device,
        mesh=mesh,
        in_specs=(
            P(("tile", "clip"), None),
            P(("tile", "clip")),
            P(("tile", "clip")),
            P(),
            P(),
            P(),
            P(),
            P(),
        ),
        out_specs=P("clip", "tile", None, None, None, None),
        check_vma=False,
    )
```

profile of v0, /device:TPU:0, one launch (start us, length us, event | category | flops | bytes accessed | tf_op | source)
XLA Modules:
  0.0 185.9 jit_solution(9642833911319196824)
XLA Ops:
  0.7 9.0 %reduce-window.6 = s32[32,8,128]{2,1,0:T(8,128)S(1)} reduce-window(s32[32,8,128]{2,1,0:T(8,128)S(1)} %fusion.53, s32[]{:T(128)} %constant.69.clone.1), window={size=1x1x128 pad=0_0x0_0x127_0}, to_apply=%region_0.0 | reduce-window | flops 4161536 | bytes 262148 | tf_op jit(solution)/shard_map/reduce-window
  11.6 4.5 %scatter_custom_fusion = s32[1536]{0:T(1024)S(1)} fusion(s32[1024]{0:T(1024)S(1)} %compare_select_fusion.1, s32[1024]{0:T(1024)} %param.10, s32[]{:T(128)} %constant.80.clone.1), kind=kCustom, calls=%fused_computation.106 | custom fusion | bytes 6656 | tf_op jit(solution)/shard_map/scatter | solution.py:66
  16.9 7.3 %all-to-all-start = ((s32[8,1,192]{2,1,0:T(1,128)}), s32[8,1,192]{2,1,0:T(1,128)S(1)}, u32[]{:S(2)}, u32[]{:S(2)}) async-start(s32[8,1,192]{2,1,0:T(1,128)} %reshape.525), calls=%async_computation | async-start | bytes 16384 | tf_op jit(solution)/shard_map/all_to_all | solution.py:79
  24.1 6.0 %scatter_custom_fusion.1 = bf16[1536,512]{1,0:T(8,128)(2,1)S(1)} fusion(s32[1024]{0:T(1024)S(1)} %compare_select_fusion.1, bf16[1024,512]{1,0:T(8,128)(2,1)} %param.8, bf16[]{:T(256)} %constant.79.clone.1), kind=kCustom, calls=%fused_computation.80 | custom fusion | bytes 1573376 | tf_op jit(solution)/shard_map/scatter | solution.py:63
  30.2 1.3 copy.91
  31.5 6.0 %all-to-all-start.2 = ((bf16[4,8,48,512]{3,2,0,1:T(8,128)(2,1)}), bf16[4,8,48,512]{3,2,0,1:T(8,128)(2,1)S(1)}, u32[]{:S(2)}, u32[]{:S(2)}) async-start(bf16[4,8,48,512]{3,2,0,1:T(8,128)(2,1)} %copy.91), calls=%async_computation.2 | async-start | bytes 3145728 | tf_op jit(solution)/shard_map/all_to_all | solution.py:72
  39.4 34.5 %all-to-all-done.2 = bf16[4,8,48,512]{3,2,0,1:T(8,128)(2,1)S(1)} async-done(((bf16[4,8,48,512]{3,2,0,1:T(8,128)(2,1)}), bf16[4,8,48,512]{3,2,0,1:T(8,128)(2,1)S(1)}, u32[]{:S(2)}, u32[]{:S(2)}) %all-to-all-start.2) | async-done | bytes 1572896 | tf_op jit(solution)/shard_map/all_to_all | solution.py:72
  73.9 3.2 %all-to-all-start.1 = ((s32[4,1,384]{2,1,0:T(1,128)}), s32[4,1,384]{2,1,0:T(1,128)S(1)}, u32[]{:S(2)}, u32[]{:S(2)}) async-start(s32[4,1,384]{2,1,0:T(1,128)} %reshape.527), calls=%async_computation.1 | async-start | bytes 12288 | tf_op jit(solution)/shard_map/all_to_all | solution.py:78
  79.7 1.3 all-to-all-done.1
  81.0 4.3 %all-to-all-start.3 = ((bf16[4,8,48,512]{3,2,1,0:T(8,128)(2,1)}), bf16[4,8,48,512]{3,2,1,0:T(8,128)(2,1)}, u32[]{:S(2)}, u32[]{:S(2)}) async-start(bf16[4,8,48,512]{3,2,1,0:T(8,128)(2,1)} %copy.92), calls=%async_computation.3 | async-start | bytes 3145728 | tf_op jit(solution)/shard_map/all_to_all | solution.py:71
  85.9 5.5 %fusion.67 = (bf16[1,1,512,3,256]{4,2,3,1,0:T(8,128)(2,1)}, bf16[1,1,512,3,256]{4,2,3,1,0:T(8,128)(2,1)}, bf16[1,1,512,3,256]{4,2,3,1,0:T(8,128)(2,1)}, bf16[1,1...) fusion(bf16[3,3,512,3,256]{4,2,3,1,0:T(8,128)(2,1)} %param.14), kind=kLoop, calls=%fused_computation.122 | loop fusion | bytes 14155776 | tf_op jit(solution)/shard_map/slice | solution.py:127
  91.4 1.4 copy.130
  92.8 2.4 %copy.138 = bf16[1,1,512,3,256]{2,4,3,1,0:T(8,128)(2,1)} copy(bf16[1,1,512,3,256]{4,2,3,1,0:T(8,128)(2,1)} %get-tuple-element.10) | data formatting | bytes 1572864
  95.1 2.3 %copy.137 = bf16[1,1,512,3,256]{2,4,3,1,0:T(8,128)(2,1)} copy(bf16[1,1,512,3,256]{4,2,3,1,0:T(8,128)(2,1)} %get-tuple-element.11) | data formatting | bytes 1572864
  97.4 2.3 %copy.135 = bf16[1,1,512,3,256]{2,4,3,1,0:T(8,128)(2,1)} copy(bf16[1,1,512,3,256]{4,2,3,1,0:T(8,128)(2,1)} %get-tuple-element.12) | data formatting | bytes 1572864
  100.9 1.4 copy.133
  102.3 2.3 %copy.132 = bf16[1,1,512,3,256]{2,4,3,1,0:T(8,128)(2,1)} copy(bf16[1,1,512,3,256]{4,2,3,1,0:T(8,128)(2,1)} %get-tuple-element.15) | data formatting | bytes 1572864
  104.6 2.3 %copy.131 = bf16[1,1,512,3,256]{2,4,3,1,0:T(8,128)(2,1)} copy(bf16[1,1,512,3,256]{4,2,3,1,0:T(8,128)(2,1)} %get-tuple-element.16) | data formatting | bytes 1572864
  109.7 8.0 %scatter_custom_fusion.2 = bf16[1024,512]{1,0:T(8,128)(2,1)S(1)} fusion(s32[1536]{0:T(1024)S(1)} %fusion.54, bf16[1536,512]{1,0:T(8,128)(2,1)} %bitcast.5, bf16[]{:T(256)} %constant.79.clone.1), kind=kCustom, calls=%fused_computation.82 | custom fusion | bytes 1049088 | tf_op jit(solution)/shard_map/scatter | solution.py:89
  118.7 3.3 %collective-permute-start = (bf16[4,8,1,512]{3,2,1,0:T(2,128)(2,1)S(1)}, bf16[4,8,1,512]{3,2,1,0:T(2,128)(2,1)S(1)}, u32[]{:S(2)}, u32[]{:S(2)}) collective-permute-start(bf16[4,8,1,512]{3,2,1,0:T(2,128)(2,1)S(1)} %get-tuple-element.20), channel_id=1, source_target_pairs={{0,4},{4,8},{8,12},{12,16},{16,20},{20,24},{24,28},{1,5},{5,9},{9,... | collective-permute-start | bytes 98312 | tf_op jit(solution)/shard_map/ppermute | solution.py:18
  122.7 1.3 collective-permute-start.1
  124.0 20.7 %all-reduce.1 = (f32[32]{0:T(128)S(1)}, f32[32]{0:T(128)S(1)}) all-reduce(f32[32]{0:T(128)S(1)} %reduce_sum.28, f32[32]{0:T(128)S(1)} %reduce_sum.29), channel_id=1, replica_groups=mesh['tile'=8,'clip'=4] {'tile'}, use_global_device_ids=true, to_apply=%region_7.8 | all-reduce | flops 64 | bytes 512 | tf_op jit(solution)/shard_map/psum | solution.py:103
  145.0 1.3 collective-permute-start.2
  146.3 1.3 collective-permute-start.3
  149.1 6.4 %collective-permute-done.3 = bf16[4,1,34,512]{3,2,1,0:T(8,128)(2,1)S(1)} collective-permute-done((bf16[4,1,34,512]{3,2,1,0:T(8,128)(2,1)S(1)}, bf16[4,1,34,512]{3,2,1,0:T(8,128)(2,1)S(1)}, u32[]{:S(2)}, u32[]{:S(2)}) %collective-permute-start.3) | collective-permute-done | bytes 139296 | tf_op jit(solution)/shard_map/ppermute | solution.py:18
  155.5 2.5 %select_convert_fusion = bf16[4,10,34,512]{3,2,1,0:T(8,128)(2,1)S(1)} fusion(bf16[4,1,34,512]{3,2,1,0:T(8,128)(2,1)S(1)} %collective-permute-done.3, bf16[4,8,1,512]{3,2,1,0:T(2,128)(2,1)S(1)} %broadcast_select_fusion, bf16[4,8,32,512]{3,2,1,0:T(8,128)(2,1)S(1)} %bitcast.241, bf16[4,8,1,512]{3,2,1,0:T(2,128)(2,1)S(1)} %broadcast_select_fusion.1, ...), kind=kLoop, calls=%fused_computation.3 | loop fusion | flops 13926400 | bytes 2793812 | tf_op jit(solution)/shard_map/convert_element_type | solution.py:119
  158.0 2.5 %fusion.21 = f32[4,8,34,3,256]{4,2,1,0,3:T(8,128)S(1)} fusion(bf16[4,10,34,512]{3,2,1,0:T(8,128)(2,1)S(1)} %select_convert_fusion, bf16[1,1,512,3,256]{2,4,3,1,0:T(8,128)(2,1)} %copy.139), kind=kOutput, calls=%fused_computation.26 | convolution fusion | flops 855638016 | bytes 5439488 | tf_op jit(solution)/shard_map/dot_general | solution.py:128
  165.6 3.1 %fusion.19 = f32[4,8,34,3,256]{4,2,3,1,0:T(8,128)} fusion(bf16[4,10,34,512]{3,2,1,0:T(8,128)(2,1)S(1)} %select_convert_fusion, bf16[1,1,512,3,256]{2,4,3,1,0:T(8,128)(2,1)S(1)} %copy-done), kind=kOutput, calls=%fused_computation.24 | convolution fusion | flops 855638016 | bytes 5521408 | tf_op jit(solution)/shard_map/dot_general | solution.py:128
  168.7 3.2 %fusion.23 = f32[4,8,34,3,256]{4,2,1,0,3:T(8,128)} fusion(bf16[4,10,34,512]{3,2,1,0:T(8,128)(2,1)S(1)} %select_convert_fusion, bf16[1,1,512,3,256]{2,4,3,1,0:T(8,128)(2,1)S(1)} %copy-done.5), kind=kOutput, calls=%fused_computation.30 | convolution fusion | flops 855638016 | bytes 5439488 | tf_op jit(solution)/shard_map/dot_general | solution.py:128
  171.9 3.2 %fusion.22 = f32[4,8,34,3,256]{4,2,1,0,3:T(8,128)} fusion(bf16[4,10,34,512]{3,2,1,0:T(8,128)(2,1)S(1)} %select_convert_fusion, bf16[1,1,512,3,256]{2,4,3,1,0:T(8,128)(2,1)S(1)} %copy-done.4), kind=kOutput, calls=%fused_computation.28 | convolution fusion | flops 855638016 | bytes 5439488 | tf_op jit(solution)/shard_map/dot_general | solution.py:128
  175.1 3.2 %fusion.4 = f32[4,8,34,3,256]{4,2,3,1,0:T(8,128)} fusion(bf16[4,10,34,512]{3,2,1,0:T(8,128)(2,1)S(1)} %select_convert_fusion, bf16[1,1,512,3,256]{2,4,3,1,0:T(8,128)(2,1)S(1)} %copy.130), kind=kOutput, calls=%fused_computation.14 | convolution fusion | flops 855638016 | bytes 5521408 | tf_op jit(solution)/shard_map/dot_general | solution.py:128
  178.3 7.6 %fusion.27 = bf16[1,1,4,8,32,256]{5,4,3,2,1,0:T(8,128)(2,1)} fusion(f32[4,8,34,3,256]{4,2,1,0,3:T(8,128)S(1)} %fusion.21, f32[4,8,34,3,256]{4,2,1,0,3:T(8,128)} %fusion.22, f32[4,8,34,3,256]{4,2,1,0,3:T(8,128)} %fusion.23, f32[4,8,34,3,256]{4,2,3,1,0:T(8,128)} %fusion.19, f32[4,8,34,3,256]{4,2,3,1,0:T(8,128)S(1)} %fusion.16, ...), kind=kLoop, calls=%fused_computation.35 | loop fusion | flops 7602176 | bytes 28836868 | tf_op jit(solution)/shard_map/convert_element_type | solution.py:133
  (75 shorter events, 20.1 us)
Async XLA Ops:
  16.9 14.6 %all-to-all-start = ((s32[8,1,192]{2,1,0:T(1,128)}), s32[8,1,192]{2,1,0:T(1,128)S(1)}, u32[]{:S(2)}, u32[]{:S(2)}) async-start(s32[8,1,192]{2,1,0:T(1,128)} %reshape.525), calls=%async_computation | async-start | bytes 16384 | tf_op jit(solution)/shard_map/all_to_all | solution.py:79
  30.2 47.0 %copy-start.9 = (s32[4]{0:T(128)S(1)}, s32[4]{0:T(128)}, u32[]{:S(2)}) copy-start(s32[4]{0:T(128)} %param.11) | copy-start | bytes 52
  31.5 42.4 %all-to-all-start.2 = ((bf16[4,8,48,512]{3,2,0,1:T(8,128)(2,1)}), bf16[4,8,48,512]{3,2,0,1:T(8,128)(2,1)S(1)}, u32[]{:S(2)}, u32[]{:S(2)}) async-start(bf16[4,8,48,512]{3,2,0,1:T(8,128)(2,1)} %copy.91), calls=%async_computation.2 | async-start | bytes 3145728 | tf_op jit(solution)/shard_map/all_to_all | solution.py:72
  73.9 7.0 %all-to-all-start.1 = ((s32[4,1,384]{2,1,0:T(1,128)}), s32[4,1,384]{2,1,0:T(1,128)S(1)}, u32[]{:S(2)}, u32[]{:S(2)}) async-start(s32[4,1,384]{2,1,0:T(1,128)} %reshape.527), calls=%async_computation.1 | async-start | bytes 12288 | tf_op jit(solution)/shard_map/all_to_all | solution.py:78
  81.0 28.7 %all-to-all-start.3 = ((bf16[4,8,48,512]{3,2,1,0:T(8,128)(2,1)}), bf16[4,8,48,512]{3,2,1,0:T(8,128)(2,1)}, u32[]{:S(2)}, u32[]{:S(2)}) async-start(bf16[4,8,48,512]{3,2,1,0:T(8,128)(2,1)} %copy.92), calls=%async_computation.3 | async-start | bytes 3145728 | tf_op jit(solution)/shard_map/all_to_all | solution.py:71
  109.7 45.9 %copy-start.6 = (f32[512]{0:T(512)S(1)}, f32[512]{0:T(512)}, u32[]{:S(2)}) copy-start(f32[512]{0:T(512)} %param.13) | copy-start | bytes 6148
  109.7 45.9 %copy-start.7 = (f32[512]{0:T(512)S(1)}, f32[512]{0:T(512)}, u32[]{:S(2)}) copy-start(f32[512]{0:T(512)} %param.12) | copy-start | bytes 6148
  118.7 26.0 %collective-permute-start = (bf16[4,8,1,512]{3,2,1,0:T(2,128)(2,1)S(1)}, bf16[4,8,1,512]{3,2,1,0:T(2,128)(2,1)S(1)}, u32[]{:S(2)}, u32[]{:S(2)}) collective-permute-start(bf16[4,8,1,512]{3,2,1,0:T(2,128)(2,1)S(1)} %get-tuple-element.20), channel_id=1, source_target_pairs={{0,4},{4,8},{8,12},{12,16},{16,20},{20,24},{24,28},{1,5},{5,9},{9,... | collective-permute-start | bytes 98312 | tf_op jit(solution)/shard_map/ppermute | solution.py:18
  122.7 22.1 %collective-permute-start.1 = (bf16[4,8,1,512]{3,2,1,0:T(2,128)(2,1)S(1)}, bf16[4,8,1,512]{3,2,1,0:T(2,128)(2,1)S(1)}, u32[]{:S(2)}, u32[]{:S(2)}) collective-permute-start(bf16[4,8,1,512]{3,2,1,0:T(2,128)(2,1)S(1)} %get-tuple-element.21), channel_id=1, source_target_pairs={{4,0},{8,4},{12,8},{16,12},{20,16},{24,20},{28,24},{5,1},{9,5},{13... | collective-permute-start | bytes 98312 | tf_op jit(solution)/shard_map/ppermute | solution.py:18
  145.0 4.2 %collective-permute-start.2 = (bf16[4,1,34,512]{3,2,1,0:T(8,128)(2,1)S(1)}, bf16[4,1,34,512]{3,2,1,0:T(8,128)(2,1)S(1)}, u32[]{:S(2)}, u32[]{:S(2)}) collective-permute-start(bf16[4,1,34,512]{3,2,1,0:T(8,128)(2,1)S(1)} %get-tuple-element.18), channel_id=1, source_target_pairs={{0,16},{4,20},{8,24},{12,28},{1,17},{5,21},{9,25},{13,29},{2,18},{... | collective-permute-start | bytes 417800 | tf_op jit(solution)/shard_map/ppermute | solution.py:18
  146.3 9.2 %collective-permute-start.3 = (bf16[4,1,34,512]{3,2,1,0:T(8,128)(2,1)S(1)}, bf16[4,1,34,512]{3,2,1,0:T(8,128)(2,1)S(1)}, u32[]{:S(2)}, u32[]{:S(2)}) collective-permute-start(bf16[4,1,34,512]{3,2,1,0:T(8,128)(2,1)S(1)} %get-tuple-element.19), channel_id=1, source_target_pairs={{16,0},{20,4},{24,8},{28,12},{17,1},{21,5},{25,9},{29,13},{18,2},{... | collective-permute-start | bytes 417800 | tf_op jit(solution)/shard_map/ppermute | solution.py:18
  158.0 2.5 %copy-start.3 = (bf16[1,1,512,3,256]{2,4,3,1,0:T(8,128)(2,1)S(1)}, bf16[1,1,512,3,256]{2,4,3,1,0:T(8,128)(2,1)}, u32[]{:S(2)}) copy-start(bf16[1,1,512,3,256]{2,4,3,1,0:T(8,128)(2,1)} %copy.131) | copy-start | bytes 2359300
  160.5 1.3 copy-start.2
  163.0 1.3 copy-start.1
  164.3 1.3 copy-start
  165.6 3.2 %copy-start.5 = (bf16[1,1,512,3,256]{2,4,3,1,0:T(8,128)(2,1)S(1)}, bf16[1,1,512,3,256]{2,4,3,1,0:T(8,128)(2,1)}, u32[]{:S(2)}) copy-start(bf16[1,1,512,3,256]{2,4,3,1,0:T(8,128)(2,1)} %copy.137) | copy-start | bytes 2359300
  168.7 3.2 %copy-start.4 = (bf16[1,1,512,3,256]{2,4,3,1,0:T(8,128)(2,1)S(1)}, bf16[1,1,512,3,256]{2,4,3,1,0:T(8,128)(2,1)}, u32[]{:S(2)}) copy-start(bf16[1,1,512,3,256]{2,4,3,1,0:T(8,128)(2,1)} %copy.138) | copy-start | bytes 2359300
  175.1 3.2 %copy-start.8 = (f32[256]{0:T(256)S(1)}, f32[256]{0:T(256)}, u32[]{:S(2)}) copy-start(f32[256]{0:T(256)} %param.15) | copy-start | bytes 3076
where the time goes:
time: 187 us; the launch traced here: 186 us
  local copies, waits for them, and re-layouts  47 us (25%)
  waiting for transfers between devices  43.4 us (23%)
  starting transfers between devices  28.1 us (15%)
  other arithmetic  24.4 us (13%)
  matrix products  21.3 us (11%)
  blocking collectives  20.7 us (11%)
    all_to_all x1, waiting for transfers between devices, on_device(): lax.all_to_all(outgoing, 'tile', split_axis=1, concat_axis=1, tiled=True)  34.5 us
    psum x1, blocking collectives, on_device(): first_sum, second_sum = lax.psum((first_sum, second_sum), 'tile')  20.7 us
    dot_general x9, matrix products, on_device(): product = jnp.dot(slab_rows, kernel, preferred_element_type=jnp.float32)  20.2 us
    unnamed x33, local copies, waits for them, and re-layouts  18.3 us
    another operation x2, other arithmetic  9.04 us
    scatter x1, local copies, waits for them, and re-layouts, on_device(): tile_rows = jnp.zeros((row_count, channels), jnp.bfloat16).at[arrived_slo...  8 us
    ppermute x4, waiting for transfers between devices, shifted(): return lax.ppermute(block, axis, route)  7.63 us
    convert_element_type x1, other arithmetic, on_device(): return decoded.astype(jnp.bfloat16)[None, None]  7.58 us
  transfers between devices with their start and end apart: 8, of which 4 were waited for; matrix products, arithmetic and copies ran while one was open for 20% of the time, Pallas kernels for 0%

commit v1 on v0

--- a/solution.py
+++ b/solution.py
@@ -10,6 +10,12 @@
 GW = 4
 EPSILON = 1e-06
 HIGHEST = lax.Precision.HIGHEST
+
+
+def stacked_exchange(array, mesh_axis, split, join):
+    cells = jnp.split(array, lax.axis_size(mesh_axis), axis=split)
+    got = lax.all_to_all(jnp.stack(cells), mesh_axis, 0, 0)
+    return jnp.concatenate(got, axis=join)
 
 
 def shifted(block, axis, distance):
@@ -76,7 +82,7 @@
             tiled=True,
         ),
         lax.all_to_all(
-            lax.all_to_all(slot_list, "tile", split_axis=1, concat_axis=1, tiled=True),
+            stacked_exchange(slot_list, "tile", 1, 1),
             "clip",
             split_axis=0,
             concat_axis=0,

time: 187 us -> 187 us (level)
    unnamed x33 -> x40, local copies, waits for them, and re-layouts: 18.3 us -> 18.4 us
where the time goes in v1:
time: 187 us; the launch traced here: 186 us
  local copies, waits for them, and re-layouts  47.1 us (25%)
  waiting for transfers between devices  43.4 us (23%)
  starting transfers between devices  28.2 us (15%)
  other arithmetic  24.4 us (13%)
  matrix products  21.3 us (11%)
  blocking collectives  20.7 us (11%)
    all_to_all x1, waiting for transfers between devices, on_device(): lax.all_to_all(outgoing, 'tile', split_axis=1, concat_axis=1, tiled=True)  34.5 us
    psum x1, blocking collectives, on_device(): first_sum, second_sum = lax.psum((first_sum, second_sum), 'tile')  20.7 us
    dot_general x9, matrix products, on_device(): product = jnp.dot(slab_rows, kernel, preferred_element_type=jnp.float32)  20.1 us
    unnamed x40, local copies, waits for them, and re-layouts  18.4 us
    another operation x2, other arithmetic  9.04 us
    scatter x1, local copies, waits for them, and re-layouts, on_device(): tile_rows = jnp.zeros((row_count, channels), jnp.bfloat16).at[arrived_slo...  8 us
    ppermute x4, waiting for transfers between devices, shifted(): return lax.ppermute(block, axis, route)  7.63 us
    convert_element_type x1, other arithmetic, on_device(): return decoded.astype(jnp.bfloat16)[None, None]  7.58 us
  transfers between devices with their start and end apart: 8, of which 4 were waited for; matrix products, arithmetic and copies ran while one was open for 20% of the time, Pallas kernels for 0%

profile of v1, /device:TPU:0, one launch (start us, length us, event | category | flops | bytes accessed | tf_op | source)
XLA Modules:
  0.0 186.1 jit_solution(14362057971189687317)
XLA Ops:
  0.7 9.0 %reduce-window.6 = s32[32,8,128]{2,1,0:T(8,128)S(1)} reduce-window(s32[32,8,128]{2,1,0:T(8,128)S(1)} %fusion.53, s32[]{:T(128)} %constant.69.clone.1), window={size=1x1x128 pad=0_0x0_0x127_0}, to_apply=%region_0.0 | reduce-window | flops 4161536 | bytes 262148 | tf_op jit(solution)/shard_map/reduce-window
  11.6 4.5 %scatter_custom_fusion = s32[1536]{0:T(1024)S(1)} fusion(s32[1024]{0:T(1024)S(1)} %compare_select_fusion.1, s32[1024]{0:T(1024)} %param.10, s32[]{:T(128)} %constant.80.clone.1), kind=kCustom, calls=%fused_computation.114 | custom fusion | bytes 6656 | tf_op jit(solution)/shard_map/scatter | solution.py:72
  17.0 7.3 %all-to-all-start = ((s32[8,1,192]{2,1,0:T(1,128)}), s32[8,1,192]{2,1,0:T(1,128)S(1)}, u32[]{:S(2)}, u32[]{:S(2)}) async-start(s32[8,1,192]{2,1,0:T(1,128)} %reshape.533), calls=%async_computation | async-start | bytes 16384 | tf_op jit(solution)/shard_map/all_to_all | solution.py:17
  24.2 6.0 %scatter_custom_fusion.1 = bf16[1536,512]{1,0:T(8,128)(2,1)S(1)} fusion(s32[1024]{0:T(1024)S(1)} %compare_select_fusion.1, bf16[1024,512]{1,0:T(8,128)(2,1)} %param.8, bf16[]{:T(256)} %constant.79.clone.1), kind=kCustom, calls=%fused_computation.80 | custom fusion | bytes 1573376 | tf_op jit(solution)/shard_map/scatter | solution.py:69
  30.3 1.3 copy.123
  31.6 6.1 %all-to-all-start.2 = ((bf16[4,8,48,512]{3,2,0,1:T(8,128)(2,1)}), bf16[4,8,48,512]{3,2,0,1:T(8,128)(2,1)S(1)}, u32[]{:S(2)}, u32[]{:S(2)}) async-start(bf16[4,8,48,512]{3,2,0,1:T(8,128)(2,1)} %copy.123), calls=%async_computation.2 | async-start | bytes 3145728 | tf_op jit(solution)/shard_map/all_to_all | solution.py:78
  39.7 34.5 %all-to-all-done.2 = bf16[4,8,48,512]{3,2,0,1:T(8,128)(2,1)S(1)} async-done(((bf16[4,8,48,512]{3,2,0,1:T(8,128)(2,1)}), bf16[4,8,48,512]{3,2,0,1:T(8,128)(2,1)S(1)}, u32[]{:S(2)}, u32[]{:S(2)}) %all-to-all-start.2) | async-done | bytes 1572896 | tf_op jit(solution)/shard_map/all_to_all | solution.py:78
  74.2 3.2 %all-to-all-start.1 = ((s32[4,1,384]{2,1,0:T(1,128)}), s32[4,1,384]{2,1,0:T(1,128)S(1)}, u32[]{:S(2)}, u32[]{:S(2)}) async-start(s32[4,1,384]{2,1,0:T(1,128)} %reshape.535), calls=%async_computation.1 | async-start | bytes 12288 | tf_op jit(solution)/shard_map/all_to_all | solution.py:84
  79.9 1.3 all-to-all-done.1
  81.2 4.3 %all-to-all-start.3 = ((bf16[4,8,48,512]{3,2,1,0:T(8,128)(2,1)}), bf16[4,8,48,512]{3,2,1,0:T(8,128)(2,1)}, u32[]{:S(2)}, u32[]{:S(2)}) async-start(bf16[4,8,48,512]{3,2,1,0:T(8,128)(2,1)} %copy.124), calls=%async_computation.3 | async-start | bytes 3145728 | tf_op jit(solution)/shard_map/all_to_all | solution.py:77
  86.1 5.5 %fusion.67 = (bf16[1,1,512,3,256]{4,2,3,1,0:T(8,128)(2,1)}, bf16[1,1,512,3,256]{4,2,3,1,0:T(8,128)(2,1)}, bf16[1,1,512,3,256]{4,2,3,1,0:T(8,128)(2,1)}, bf16[1,1...) fusion(bf16[3,3,512,3,256]{4,2,3,1,0:T(8,128)(2,1)} %param.14), kind=kLoop, calls=%fused_computation.130 | loop fusion | bytes 14155776 | tf_op jit(solution)/shard_map/slice | solution.py:133
  91.6 1.4 copy.169
  93.0 2.4 %copy.177 = bf16[1,1,512,3,256]{2,4,3,1,0:T(8,128)(2,1)} copy(bf16[1,1,512,3,256]{4,2,3,1,0:T(8,128)(2,1)} %get-tuple-element.10) | data formatting | bytes 1572864
  95.4 2.3 %copy.176 = bf16[1,1,512,3,256]{2,4,3,1,0:T(8,128)(2,1)} copy(bf16[1,1,512,3,256]{4,2,3,1,0:T(8,128)(2,1)} %get-tuple-element.11) | data formatting | bytes 1572864
  97.7 2.3 %copy.174 = bf16[1,1,512,3,256]{2,4,3,1,0:T(8,128)(2,1)} copy(bf16[1,1,512,3,256]{4,2,3,1,0:T(8,128)(2,1)} %get-tuple-element.12) | data formatting | bytes 1572864
  101.1 1.4 copy.172
  102.5 2.3 %copy.171 = bf16[1,1,512,3,256]{2,4,3,1,0:T(8,128)(2,1)} copy(bf16[1,1,512,3,256]{4,2,3,1,0:T(8,128)(2,1)} %get-tuple-element.15) | data formatting | bytes 1572864
  104.8 2.3 %copy.170 = bf16[1,1,512,3,256]{2,4,3,1,0:T(8,128)(2,1)} copy(bf16[1,1,512,3,256]{4,2,3,1,0:T(8,128)(2,1)} %get-tuple-element.16) | data formatting | bytes 1572864
  109.9 8.0 %scatter_custom_fusion.2 = bf16[1024,512]{1,0:T(8,128)(2,1)S(1)} fusion(s32[1536]{0:T(1024)S(1)} %fusion.54, bf16[1536,512]{1,0:T(8,128)(2,1)} %bitcast.15, bf16[]{:T(256)} %constant.79.clone.1), kind=kCustom, calls=%fused_computation.82 | custom fusion | bytes 1049088 | tf_op jit(solution)/shard_map/scatter | solution.py:95
  118.9 3.3 %collective-permute-start = (bf16[4,8,1,512]{3,2,1,0:T(2,128)(2,1)S(1)}, bf16[4,8,1,512]{3,2,1,0:T(2,128)(2,1)S(1)}, u32[]{:S(2)}, u32[]{:S(2)}) collective-permute-start(bf16[4,8,1,512]{3,2,1,0:T(2,128)(2,1)S(1)} %get-tuple-element.20), channel_id=1, source_target_pairs={{0,4},{4,8},{8,12},{12,16},{16,20},{20,24},{24,28},{1,5},{5,9},{9,... | collective-permute-start | bytes 98312 | tf_op jit(solution)/shard_map/ppermute | solution.py:24
  122.9 1.3 collective-permute-start.1
  124.2 20.7 %all-reduce.1 = (f32[32]{0:T(128)S(1)}, f32[32]{0:T(128)S(1)}) all-reduce(f32[32]{0:T(128)S(1)} %reduce_sum.28, f32[32]{0:T(128)S(1)} %reduce_sum.29), channel_id=1, replica_groups=mesh['tile'=8,'clip'=4] {'tile'}, use_global_device_ids=true, to_apply=%region_7.8 | all-reduce | flops 64 | bytes 512 | tf_op jit(solution)/shard_map/psum | solution.py:109
  145.2 1.3 collective-permute-start.2
  146.5 1.3 collective-permute-start.3
  149.4 6.4 %collective-permute-done.3 = bf16[4,1,34,512]{3,2,1,0:T(8,128)(2,1)S(1)} collective-permute-done((bf16[4,1,34,512]{3,2,1,0:T(8,128)(2,1)S(1)}, bf16[4,1,34,512]{3,2,1,0:T(8,128)(2,1)S(1)}, u32[]{:S(2)}, u32[]{:S(2)}) %collective-permute-start.3) | collective-permute-done | bytes 139296 | tf_op jit(solution)/shard_map/ppermute | solution.py:24
  155.8 2.5 %select_convert_fusion = bf16[4,10,34,512]{3,2,1,0:T(8,128)(2,1)S(1)} fusion(bf16[4,1,34,512]{3,2,1,0:T(8,128)(2,1)S(1)} %collective-permute-done.3, bf16[4,8,1,512]{3,2,1,0:T(2,128)(2,1)S(1)} %broadcast_select_fusion, bf16[4,8,32,512]{3,2,1,0:T(8,128)(2,1)S(1)} %bitcast.266, bf16[4,8,1,512]{3,2,1,0:T(2,128)(2,1)S(1)} %broadcast_select_fusion.1, ...), kind=kLoop, calls=%fused_computation.3 | loop fusion | flops 13926400 | bytes 2793812 | tf_op jit(solution)/shard_map/convert_element_type | solution.py:125
  158.3 2.5 %fusion.21 = f32[4,8,34,3,256]{4,2,1,0,3:T(8,128)S(1)} fusion(bf16[4,10,34,512]{3,2,1,0:T(8,128)(2,1)S(1)} %select_convert_fusion, bf16[1,1,512,3,256]{2,4,3,1,0:T(8,128)(2,1)} %copy.178), kind=kOutput, calls=%fused_computation.26 | convolution fusion | flops 855638016 | bytes 5439488 | tf_op jit(solution)/shard_map/dot_general | solution.py:134
  165.8 3.1 %fusion.19 = f32[4,8,34,3,256]{4,2,3,1,0:T(8,128)} fusion(bf16[4,10,34,512]{3,2,1,0:T(8,128)(2,1)S(1)} %select_convert_fusion, bf16[1,1,512,3,256]{2,4,3,1,0:T(8,128)(2,1)S(1)} %copy-done), kind=kOutput, calls=%fused_computation.24 | convolution fusion | flops 855638016 | bytes 5521408 | tf_op jit(solution)/shard_map/dot_general | solution.py:134
  168.9 3.1 %fusion.23 = f32[4,8,34,3,256]{4,2,1,0,3:T(8,128)} fusion(bf16[4,10,34,512]{3,2,1,0:T(8,128)(2,1)S(1)} %select_convert_fusion, bf16[1,1,512,3,256]{2,4,3,1,0:T(8,128)(2,1)S(1)} %copy-done.5), kind=kOutput, calls=%fused_computation.30 | convolution fusion | flops 855638016 | bytes 5439488 | tf_op jit(solution)/shard_map/dot_general | solution.py:134
  172.1 3.2 %fusion.22 = f32[4,8,34,3,256]{4,2,1,0,3:T(8,128)} fusion(bf16[4,10,34,512]{3,2,1,0:T(8,128)(2,1)S(1)} %select_convert_fusion, bf16[1,1,512,3,256]{2,4,3,1,0:T(8,128)(2,1)S(1)} %copy-done.4), kind=kOutput, calls=%fused_computation.28 | convolution fusion | flops 855638016 | bytes 5439488 | tf_op jit(solution)/shard_map/dot_general | solution.py:134
  175.3 3.2 %fusion.4 = f32[4,8,34,3,256]{4,2,3,1,0:T(8,128)} fusion(bf16[4,10,34,512]{3,2,1,0:T(8,128)(2,1)S(1)} %select_convert_fusion, bf16[1,1,512,3,256]{2,4,3,1,0:T(8,128)(2,1)S(1)} %copy.169), kind=kOutput, calls=%fused_computation.14 | convolution fusion | flops 855638016 | bytes 5521408 | tf_op jit(solution)/shard_map/dot_general | solution.py:134
  178.5 7.6 %fusion.27 = bf16[1,1,4,8,32,256]{5,4,3,2,1,0:T(8,128)(2,1)} fusion(f32[4,8,34,3,256]{4,2,1,0,3:T(8,128)S(1)} %fusion.21, f32[4,8,34,3,256]{4,2,1,0,3:T(8,128)} %fusion.22, f32[4,8,34,3,256]{4,2,1,0,3:T(8,128)} %fusion.23, f32[4,8,34,3,256]{4,2,3,1,0:T(8,128)} %fusion.19, f32[4,8,34,3,256]{4,2,3,1,0:T(8,128)S(1)} %fusion.16, ...), kind=kLoop, calls=%fused_computation.35 | loop fusion | flops 7602176 | bytes 28836868 | tf_op jit(solution)/shard_map/convert_element_type | solution.py:139
  (84 shorter events, 20.1 us)
Async XLA Ops:
  17.0 14.6 %all-to-all-start = ((s32[8,1,192]{2,1,0:T(1,128)}), s32[8,1,192]{2,1,0:T(1,128)S(1)}, u32[]{:S(2)}, u32[]{:S(2)}) async-start(s32[8,1,192]{2,1,0:T(1,128)} %reshape.533), calls=%async_computation | async-start | bytes 16384 | tf_op jit(solution)/shard_map/all_to_all | solution.py:17
  31.6 45.9 %copy-start.9 = (s32[4]{0:T(128)S(1)}, s32[4]{0:T(128)}, u32[]{:S(2)}) copy-start(s32[4]{0:T(128)} %param.11) | copy-start | bytes 52
  31.6 42.6 %all-to-all-start.2 = ((bf16[4,8,48,512]{3,2,0,1:T(8,128)(2,1)}), bf16[4,8,48,512]{3,2,0,1:T(8,128)(2,1)S(1)}, u32[]{:S(2)}, u32[]{:S(2)}) async-start(bf16[4,8,48,512]{3,2,0,1:T(8,128)(2,1)} %copy.123), calls=%async_computation.2 | async-start | bytes 3145728 | tf_op jit(solution)/shard_map/all_to_all | solution.py:78
  74.2 7.0 %all-to-all-start.1 = ((s32[4,1,384]{2,1,0:T(1,128)}), s32[4,1,384]{2,1,0:T(1,128)S(1)}, u32[]{:S(2)}, u32[]{:S(2)}) async-start(s32[4,1,384]{2,1,0:T(1,128)} %reshape.535), calls=%async_computation.1 | async-start | bytes 12288 | tf_op jit(solution)/shard_map/all_to_all | solution.py:84
  81.2 28.7 %all-to-all-start.3 = ((bf16[4,8,48,512]{3,2,1,0:T(8,128)(2,1)}), bf16[4,8,48,512]{3,2,1,0:T(8,128)(2,1)}, u32[]{:S(2)}, u32[]{:S(2)}) async-start(bf16[4,8,48,512]{3,2,1,0:T(8,128)(2,1)} %copy.124), calls=%async_computation.3 | async-start | bytes 3145728 | tf_op jit(solution)/shard_map/all_to_all | solution.py:77
  109.9 45.9 %copy-start.6 = (f32[512]{0:T(512)S(1)}, f32[512]{0:T(512)}, u32[]{:S(2)}) copy-start(f32[512]{0:T(512)} %param.13) | copy-start | bytes 6148
  109.9 45.9 %copy-start.7 = (f32[512]{0:T(512)S(1)}, f32[512]{0:T(512)}, u32[]{:S(2)}) copy-start(f32[512]{0:T(512)} %param.12) | copy-start | bytes 6148
  118.9 26.0 %collective-permute-start = (bf16[4,8,1,512]{3,2,1,0:T(2,128)(2,1)S(1)}, bf16[4,8,1,512]{3,2,1,0:T(2,128)(2,1)S(1)}, u32[]{:S(2)}, u32[]{:S(2)}) collective-permute-start(bf16[4,8,1,512]{3,2,1,0:T(2,128)(2,1)S(1)} %get-tuple-element.20), channel_id=1, source_target_pairs={{0,4},{4,8},{8,12},{12,16},{16,20},{20,24},{24,28},{1,5},{5,9},{9,... | collective-permute-start | bytes 98312 | tf_op jit(solution)/shard_map/ppermute | solution.py:24
  122.9 22.1 %collective-permute-start.1 = (bf16[4,8,1,512]{3,2,1,0:T(2,128)(2,1)S(1)}, bf16[4,8,1,512]{3,2,1,0:T(2,128)(2,1)S(1)}, u32[]{:S(2)}, u32[]{:S(2)}) collective-permute-start(bf16[4,8,1,512]{3,2,1,0:T(2,128)(2,1)S(1)} %get-tuple-element.21), channel_id=1, source_target_pairs={{4,0},{8,4},{12,8},{16,12},{20,16},{24,20},{28,24},{5,1},{9,5},{13... | collective-permute-start | bytes 98312 | tf_op jit(solution)/shard_map/ppermute | solution.py:24
  145.2 4.2 %collective-permute-start.2 = (bf16[4,1,34,512]{3,2,1,0:T(8,128)(2,1)S(1)}, bf16[4,1,34,512]{3,2,1,0:T(8,128)(2,1)S(1)}, u32[]{:S(2)}, u32[]{:S(2)}) collective-permute-start(bf16[4,1,34,512]{3,2,1,0:T(8,128)(2,1)S(1)} %get-tuple-element.18), channel_id=1, source_target_pairs={{0,16},{4,20},{8,24},{12,28},{1,17},{5,21},{9,25},{13,29},{2,18},{... | collective-permute-start | bytes 417800 | tf_op jit(solution)/shard_map/ppermute | solution.py:24
  146.5 9.2 %collective-permute-start.3 = (bf16[4,1,34,512]{3,2,1,0:T(8,128)(2,1)S(1)}, bf16[4,1,34,512]{3,2,1,0:T(8,128)(2,1)S(1)}, u32[]{:S(2)}, u32[]{:S(2)}) collective-permute-start(bf16[4,1,34,512]{3,2,1,0:T(8,128)(2,1)S(1)} %get-tuple-element.19), channel_id=1, source_target_pairs={{16,0},{20,4},{24,8},{28,12},{17,1},{21,5},{25,9},{29,13},{18,2},{... | collective-permute-start | bytes 417800 | tf_op jit(solution)/shard_map/ppermute | solution.py:24
  158.3 2.5 %copy-start.3 = (bf16[1,1,512,3,256]{2,4,3,1,0:T(8,128)(2,1)S(1)}, bf16[1,1,512,3,256]{2,4,3,1,0:T(8,128)(2,1)}, u32[]{:S(2)}) copy-start(bf16[1,1,512,3,256]{2,4,3,1,0:T(8,128)(2,1)} %copy.170) | copy-start | bytes 2359300
  160.7 1.3 copy-start.2
  163.3 1.3 copy-start.1
  164.5 1.3 copy-start
  165.8 3.1 %copy-start.5 = (bf16[1,1,512,3,256]{2,4,3,1,0:T(8,128)(2,1)S(1)}, bf16[1,1,512,3,256]{2,4,3,1,0:T(8,128)(2,1)}, u32[]{:S(2)}) copy-start(bf16[1,1,512,3,256]{2,4,3,1,0:T(8,128)(2,1)} %copy.176) | copy-start | bytes 2359300
  168.9 3.1 %copy-start.4 = (bf16[1,1,512,3,256]{2,4,3,1,0:T(8,128)(2,1)S(1)}, bf16[1,1,512,3,256]{2,4,3,1,0:T(8,128)(2,1)}, u32[]{:S(2)}) copy-start(bf16[1,1,512,3,256]{2,4,3,1,0:T(8,128)(2,1)} %copy.177) | copy-start | bytes 2359300
  175.3 3.2 %copy-start.8 = (f32[256]{0:T(256)S(1)}, f32[256]{0:T(256)}, u32[]{:S(2)}) copy-start(f32[256]{0:T(256)} %param.15) | copy-start | bytes 3076
